TPU v7x, 256 devices: a whole 4x4x8 slice. The times are simulated.
256 devices in a mesh: br: 8 (over y_lo, x), bus: 32 (over y_hi, z, core).
Axes of the slice: x: 4, y: 4 (y_hi: 2, y_lo: 2; y = y_hi * 2 + y_lo), z: 8, core: 2. Of those that a mesh axis runs over, the one named last changes fastest.
Arguments:
- ptdf: bfloat16 [8192, 65536], P('br', 'bus'), may hold values from -0.0234375 to 0.0234375
- load_codes: int32 [65536, 1024], P('bus'), may hold values from -4096 to 4096
- limit_codes: int32 [8192], P('br'), may hold values from 64 to 320
Outputs:
- penalty: float32 [8192, 1024], P(('br', 'bus'))
- sensitivity: float32 [65536, 1024], P('bus', 'br')
All inputs are finite; a program needn't handle non-finite values.
Results may differ from a plain program's by a relative error of at most 0.004.
Values may be sent and summed in bfloat16 or wider, within the bound.
A program may use at most 128 MiB of HBM per device.

v0:
```python
import jax
import jax.numpy as jnp
from jax import lax
from jax.sharding import PartitionSpec as P


def overload(flows, limit_codes):
    limits = (limit_codes.astype(jnp.float32) / 64.0)[:, None]
    magnitude = jnp.sqrt(flows * flows + 1.0)
    zvalue = 4.0 * (magnitude / limits - 1.0)
    penalty = jax.nn.softplus(zvalue) / 4.0
    adjoint = (jax.nn.sigmoid(zvalue) * flows / (magnitude * limits)).astype(jnp.bfloat16)
    return (penalty, adjoint)


def local(ptdf, load_codes, limit_codes):
    injections = (load_codes.astype(jnp.float32) / 1024.0).astype(jnp.bfloat16)
    branch_local = ptdf.shape[0]
    owned = branch_local // lax.axis_size("bus")
    offset = lax.axis_index("bus") * owned
    partial_flows = jnp.dot(ptdf, injections, preferred_element_type=jnp.float32)
    flows = lax.psum(partial_flows, "bus")
    penalty_all, adjoint_block = overload(flows, limit_codes)
    penalty = lax.dynamic_slice_in_dim(penalty_all, offset, owned, 0)
    partial_sens = lax.dot_general(
        ptdf, adjoint_block, (((0,), (0,)), ((), ())), preferred_element_type=jnp.float32
    )
    sensitivity = lax.psum_scatter(partial_sens, "br", scatter_dimension=1, tiled=True)
    return (penalty, sensitivity)


def solution(mesh):
    return jax.shard_map(
        local,
        mesh=mesh,
        in_specs=(P("br", "bus"), P("bus", None), P("br")),
        out_specs=(P(("br", "bus"), None), P("bus", "br")),
        check_vma=False,
    )
```

profile of v0, /device:TPU:8, one launch (start us, length us, event | category | flops | bytes accessed | tf_op | source)
XLA Modules:
  0.0 415.1 jit_solution(15859337820836149441)
XLA Ops:
  7.2 0.0 all-reduce.2.cloned.1.call-start
  7.2 11.0 %fusion.2 = f32[1024,1024]{0,1:T(8,128)} fusion(bf16[1024,2048]{1,0:T(8,128)(2,1)} %param.3, s32[2048,1024]{1,0:T(8,128)} %param.4), kind=kOutput, calls=%fused_computation.7 | convolution fusion | flops 4301258752 | bytes 16777216 | tf_op jit(solution)/shard_map/dot_general | solution.py:21
  18.3 0.0 copy-start
  18.3 0.0 all-reduce.2.cloned.1.call-update
  18.3 0.2 reduce-scatter.2.cloned.1.call-start
  18.5 0.4 copy-done
  19.0 279.6 %all-reduce.2.cloned.1.call-done = f32[1024,1024]{0,1:T(8,128)} async-done(((f32[1024,1024]{0,1:T(8,128)}), f32[1024,1024]{0,1:T(8,128)}) %all-reduce.2.cloned.1.call-update) | async-done | bytes 4194320 | tf_op jit(solution)/shard_map/psum | solution.py:22
  298.5 13.3 %convolution_bitcast_fusion = f32[2048,1024]{0,1:T(8,128)} fusion(bf16[1024,2048]{1,0:T(8,128)(2,1)} %param.3, f32[1024,1024]{0,1:T(8,128)} %all-reduce.2.cloned.1.call-done, f32[1024]{0:T(1024)S(1)} %convert_multiply_fusion), kind=kOutput, calls=%fused_computation.1 | convolution fusion | flops 4307550208 | bytes 16781312 | tf_op jit(solution)/shard_map/dot_general | solution.py:25
  311.9 0.0 reduce-scatter.2.cloned.1.call-update
  311.9 3.9 add_multiply_fusion
  315.9 0.4 fusion.5
  316.2 0.8 copy.5
  317.1 88.7 %reduce-scatter.2.cloned.1.call-done = f32[2048,128]{0,1:T(8,128)} async-done(((f32[2048,1024]{0,1:T(8,128)}), f32[2048,128]{0,1:T(8,128)}) %reduce-scatter.2.cloned.1.call-update) | async-done | bytes 1048592 | tf_op jit(solution)/shard_map/reduce_scatter | solution.py:28
  405.7 2.5 copy.6
  (1 shorter events, 0.0 us)
Async XLA Ops:
  7.2 291.4 %all-reduce.2.cloned.1.call-start = ((), (), s32[]{:S(2)}) async-start(), calls=%async_computation.1 | async-start | bytes 8388608 | tf_op jit(solution)/shard_map/psum | solution.py:22
  18.3 0.7 copy-start
  18.3 387.5 %reduce-scatter.2.cloned.1.call-start = ((), (), s32[]{:S(2)}) async-start(), calls=%async_computation.2 | async-start | bytes 9437184 | tf_op jit(solution)/shard_map/reduce_scatter | solution.py:28
Sparse Core Ops, SparseCore 0:
  18.4 280.0 all-reduce.1
  312.0 93.6 reduce-scatter.1
where the time goes:
time: 417 us; the launch traced here: 415 us
  waiting for transfers between devices  368 us (88%)
  matrix products  24.4 us (6%)
  between operations  14.1 us (3%)
  other arithmetic  4.33 us (1%)
    psum x1, waiting for transfers between devices, local(): flows = lax.psum(partial_flows, 'bus')  280 us
    reduce_scatter x1, waiting for transfers between devices, local(): lax.psum_scatter(partial_sens, 'br', scatter_dimension=1, tiled=True)  88.7 us
    dot_general x1, matrix products, local(): lax.dot_general(ptdf, adjoint_block, (((0,), (0,)), ((), ())), preferred_...  13.3 us
    dot_general x1, matrix products, local(): jnp.dot(ptdf, injections, preferred_element_type=jnp.float32)  11 us
  transfers between devices with their start and end apart: 2, of which 2 were waited for; matrix products, arithmetic and copies ran while one was open for 1% of the time, Pallas kernels for 0%

commit v1 on v0

--- a/solution.py
+++ b/solution.py
@@ -19,9 +19,10 @@
     owned = branch_local // lax.axis_size("bus")
     offset = lax.axis_index("bus") * owned
     partial_flows = jnp.dot(ptdf, injections, preferred_element_type=jnp.float32)
-    flows = lax.psum(partial_flows, "bus")
-    penalty_all, adjoint_block = overload(flows, limit_codes)
-    penalty = lax.dynamic_slice_in_dim(penalty_all, offset, owned, 0)
+    flows = lax.psum_scatter(partial_flows, "bus", scatter_dimension=0, tiled=True)
+    limits_own = lax.dynamic_slice_in_dim(limit_codes, offset, owned, 0)
+    penalty, adjoint_own = overload(flows, limits_own)
+    adjoint_block = lax.all_gather(adjoint_own, "bus", axis=0, tiled=True)
     partial_sens = lax.dot_general(
         ptdf, adjoint_block, (((0,), (0,)), ((), ())), preferred_element_type=jnp.float32
     )

time: 417 us -> 349 us (0.84)
  waiting for transfers between devices: 368 us -> 301 us
    psum x1 -> x0, waiting for transfers between devices: 280 us -> none  [local(): flows = lax.psum(partial_flows, 'bus')]
    reduce_scatter x0 -> x1, waiting for transfers between devices: none -> 129 us  [local(): lax.psum_scatter(partial_flows, 'bus', scatter_dimension=0, tiled=True)]
    all_gather x0 -> x1, waiting for transfers between devices: none -> 79.6 us  [local(): adjoint_block = lax.all_gather(adjoint_own, 'bus', axis=0, tiled=True)]
  transfers between devices with their start and end apart: 2 -> 3, of which waited for: 2 -> 3; matrix products, arithmetic and copies ran while one was open for 1% -> 0% of each run, Pallas kernels for 0% -> 0%
where the time goes in v1:
time: 349 us; the launch traced here: 347 us
  waiting for transfers between devices  301 us (86%)
  matrix products  21.7 us (6%)
  between operations  13.7 us (4%)
  local copies, waits for them, and re-layouts  7.88 us (2%)
    reduce_scatter x1, waiting for transfers between devices, local(): lax.psum_scatter(partial_flows, 'bus', scatter_dimension=0, tiled=True)  129 us
    reduce_scatter x1, waiting for transfers between devices, local(): lax.psum_scatter(partial_sens, 'br', scatter_dimension=1, tiled=True)  91.9 us
    all_gather x1, waiting for transfers between devices, local(): adjoint_block = lax.all_gather(adjoint_own, 'bus', axis=0, tiled=True)  79.6 us
    dot_general x1, matrix products, local(): jnp.dot(ptdf, injections, preferred_element_type=jnp.float32)  11.1 us
    dot_general x1, matrix products, local(): lax.dot_general(ptdf, adjoint_block, (((0,), (0,)), ((), ())), preferred_...  10.6 us
    unnamed x2, local copies, waits for them, and re-layouts  7.88 us
  transfers between devices with their start and end apart: 3, of which 3 were waited for; matrix products, arithmetic and copies ran while one was open for 0% of the time, Pallas kernels for 0%

profile of v1, /device:TPU:8, one launch (start us, length us, event | category | flops | bytes accessed | tf_op | source)
XLA Modules:
  0.0 346.7 jit_solution(4985150040851442825)
XLA Ops:
  7.2 0.0 reduce-scatter.7.cloned.1.call-start
  7.2 11.1 %fusion.2 = f32[1024,1024]{0,1:T(8,128)} fusion(bf16[1024,2048]{1,0:T(8,128)(2,1)} %param.3, s32[2048,1024]{1,0:T(8,128)} %param.4), kind=kOutput, calls=%fused_computation.4 | convolution fusion | flops 4301258752 | bytes 16777216 | tf_op jit(solution)/shard_map/dot_general | solution.py:21
  18.3 5.3 %copy.14 = f32[1024,1024]{1,0:T(8,128)} copy(f32[1024,1024]{0,1:T(8,128)} %fusion.2) | data formatting | bytes 8388608
  23.6 0.0 reduce-scatter.7.cloned.1.call-update
  23.7 0.0 all-gather.2.cloned.1.call-start
  23.7 0.8 convert_multiply_fusion
  24.5 129.2 %reduce-scatter.7.cloned.1.call-done = f32[32,1024]{1,0:T(8,128)} async-done(((f32[1024,1024]{1,0:T(8,128)}), f32[32,1024]{1,0:T(8,128)}) %reduce-scatter.7.cloned.1.call-update) | async-done | bytes 131088 | tf_op jit(solution)/shard_map/reduce_scatter | solution.py:22
  153.7 1.8 divide_convert_fusion
  155.5 0.0 all-gather.2.cloned.1.call-update
  155.5 0.0 reduce-scatter.5.cloned.1.call-start
  155.6 79.6 %all-gather.2.cloned.1.call-done = bf16[1024,1024]{1,0:T(8,128)(2,1)} async-done(((bf16[32,1024]{1,0:T(8,128)(2,1)}), bf16[1024,1024]{1,0:T(8,128)(2,1)}) %all-gather.2.cloned.1.call-update) | async-done | bytes 2097168 | tf_op jit(solution)/shard_map/all_gather | solution.py:25
  235.2 10.6 %convolution_bitcast_fusion = f32[2048,1024]{0,1:T(8,128)} fusion(bf16[1024,1024]{1,0:T(8,128)(2,1)} %all-gather.2.cloned.1.call-done, bf16[1024,2048]{1,0:T(8,128)(2,1)} %param.3), kind=kOutput, calls=%fused_computation.1 | convolution fusion | flops 4294967296 | bytes 14680064 | tf_op jit(solution)/shard_map/dot_general | solution.py:26
  245.8 0.0 reduce-scatter.5.cloned.1.call-update
  245.8 91.9 %reduce-scatter.5.cloned.1.call-done = f32[2048,128]{0,1:T(8,128)} async-done(((f32[2048,1024]{0,1:T(8,128)}), f32[2048,128]{0,1:T(8,128)}) %reduce-scatter.5.cloned.1.call-update) | async-done | bytes 1048592 | tf_op jit(solution)/shard_map/reduce_scatter | solution.py:29
  337.7 2.5 copy.13
Async XLA Ops:
  7.2 146.5 %reduce-scatter.7.cloned.1.call-start = ((), (), s32[]{:S(2)}) async-start(), calls=%async_computation.4 | async-start | bytes 4325376 | tf_op jit(solution)/shard_map/reduce_scatter | solution.py:22
  23.7 211.5 %all-gather.2.cloned.1.call-start = ((), (), s32[]{:S(2)}) async-start(), calls=%async_computation.2 | async-start | bytes 2162688 | tf_op jit(solution)/shard_map/all_gather | solution.py:25
  155.5 182.2 %reduce-scatter.5.cloned.1.call-start = ((), (), s32[]{:S(2)}) async-start(), calls=%async_computation.3 | async-start | bytes 9437184 | tf_op jit(solution)/shard_map/reduce_scatter | solution.py:29
Sparse Core Ops, SparseCore 0:
  23.8 129.8 reduce-scatter.6
  157.4 77.7 all-gather.1
  245.9 91.7 reduce-scatter.4

commit v2 on v0

v2 whole, which is shorter than its diff:
```python
import jax
import jax.numpy as jnp
from jax import lax
from jax.experimental import pallas as pl
from jax.experimental.pallas import tpu as pltpu
from jax.sharding import PartitionSpec as P

MESH = pl.DeviceIdType.MESH
NX, NYL, NYH, NZ, NC = 4, 2, 2, 8, 2
LANES = 128
F32, BF16 = jnp.float32, jnp.bfloat16


def epilogue(flows, limits):
    magnitude = jnp.sqrt(flows * flows + 1.0)
    zvalue = 4.0 * (magnitude / limits - 1.0)
    decay = jnp.exp(-jnp.abs(zvalue))
    penalty = (jnp.maximum(zvalue, 0.0) + jnp.log1p(decay)) * 0.25
    sigmoid = jnp.where(zvalue >= 0.0, 1.0, decay) / (1.0 + decay)
    adjoint = sigmoid * flows / (magnitude * limits)
    return penalty, adjoint


def kernel(
    ptdf, codes, limits, penalty_out, sens_out,
    p_v, pt_v, codes_v, inj_v, part, core_in, y_out, y_in, z_out, z_in, z_own, adj, pen_v,
    opp_out, opp_in, right_out, left_out, right_in, left_in, pair_own, pair_out, pair_in, sens_v,
    p_sem, c_sem, core_sem, y_sem, zs_sem, zr_sem, gzs_sem, gzr_sem, gy_sem, gc_sem,
    opp_sem, right_sem, left_sem, pair_sem, pen_sem, sens_sem,
):
    br, bus = lax.axis_index("br"), lax.axis_index("bus")
    x, ylo = lax.rem(br, NX), br // NX
    core, z, yhi = lax.rem(bus, NC), lax.rem(bus // NC, NZ), bus // (NC * NZ)
    rows = p_v.shape[0]
    buses = p_v.shape[1]
    own = rows // (NYH * NZ * NC)
    width = NYL * LANES
    steps = opp_out.shape[1]
    tile = opp_out.shape[2]
    half = steps * tile

    def at_bus(h, zz, c):
        return (br, (h * NZ + zz) * NC + c)

    sibling = at_bus(yhi, z, 1 - core)
    far_y = at_bus(1 - yhi, z, core)

    def z_peer(d):
        return at_bus(yhi, lax.rem(z + d, NZ), core)

    right = (ylo * NX + lax.rem(x + 1, NX), bus)
    left = (ylo * NX + lax.rem(x + NX - 1, NX), bus)
    pair = ((1 - ylo) * NX + x, bus)
    partners = [sibling, far_y, right, left, pair] + [z_peer(d) for d in range(1, NZ)]

    def block_of(k):
        return lax.rem(x + (2, 1, 3, 0)[k], NX)

    def columns(k, b):
        return pl.ds(pl.multiple_of((block_of(k) + b * NX) * LANES, LANES), LANES)

    def remote(src, dst, send, recv, device):
        return pltpu.make_async_remote_copy(
            src_ref=src, dst_ref=dst, send_sem=send, recv_sem=recv, device_id=device, device_id_type=MESH
        )

    ptile = rows // 4

    def p_copy(i):
        s = pl.ds(i * ptile, ptile)
        return pltpu.make_async_copy(ptdf.at[s], p_v.at[s], p_sem.at[i])

    def codes_copy(k, b):
        return pltpu.make_async_copy(codes.at[:, columns(k, b)], codes_v.at[k, b], c_sem.at[k, b])

    for b in range(NYL):
        codes_copy(0, b).start()
    for i in range(4):
        p_copy(i).start()

    barrier = pltpu.get_barrier_semaphore()
    for device in partners:
        pl.semaphore_signal(barrier, inc=1, device_id=device, device_id_type=MESH)
    pl.semaphore_wait(barrier, len(partners))

    def core_copy(k):
        return remote(part.at[k, :, :, 1 - core], core_in.at[k], core_sem.at[0, k], core_sem.at[1, k], sibling)

    def y_copy(k):
        return remote(y_out.at[k], y_in.at[k], y_sem.at[0, k], y_sem.at[1, k], far_y)

    def z_copy(k, d):
        return remote(
            z_out.at[k, lax.rem(z + d, NZ)], z_in.at[k, d - 1], zs_sem.at[k, d - 1], zr_sem.at[k, d - 1], z_peer(d)
        )

    def gz_copy(k, d):
        mine = adj.at[k, yhi, z, core]
        return remote(mine, mine, gzs_sem.at[k, d - 1], gzr_sem.at[k, d - 1], z_peer(d))

    def gz_arrival(k, d):
        theirs = adj.at[k, yhi, lax.rem(z + NZ - d, NZ), core]
        return remote(theirs, theirs, gzs_sem.at[k, d - 1], gzr_sem.at[k, d - 1], z_peer(d))

    def gy_copy(k, h):
        rows_of = adj.at[k, h, :, core]
        return remote(rows_of, rows_of, gy_sem.at[0, k], gy_sem.at[1, k], far_y)

    def gc_copy(k, near, c):
        rows_of = adj.at[k, yhi if near else 1 - yhi, :, c]
        which = 0 if near else 1
        return remote(rows_of, rows_of, gc_sem.at[0, k, which], gc_sem.at[1, k, which], sibling)

    def stage_matmul(k):
        for b in range(NYL):
            codes_copy(k, b).wait()
        if k + 1 < NX:
            for b in range(NYL):
                codes_copy(k + 1, b).start()
        strip = 256

        def convert(i, _):
            s = pl.ds(pl.multiple_of(i * strip, strip), strip)
            for b in range(NYL):
                values = codes_v[k, b, s].astype(F32) * (1.0 / 1024.0)
                inj_v[s, b * LANES : (b + 1) * LANES] = values.astype(BF16)
            return 0

        lax.fori_loop(0, buses // strip, convert, 0)
        group = ptile // (NC * own)
        for i in range(4):
            if k == 0:
                p_copy(i).wait()
            product = jnp.dot(p_v[i * ptile : (i + 1) * ptile], inj_v[...], preferred_element_type=F32)
            product = product.reshape(group, NC, own, width)
            first = i * group
            part[k, first // NZ, first % NZ : first % NZ + group] = product
        core_copy(k).start()

    def stage_core(k):
        core_copy(k).wait_recv()
        y_out[k] = (part[k, 1 - yhi, :, core] + core_in[k, 1 - yhi]).astype(BF16)
        y_copy(k).start()

    def stage_y(k):
        y_copy(k).wait_recv()
        total = part[k, yhi, :, core] + core_in[k, yhi] + y_in[k].astype(F32)
        part[k, yhi, :, core] = total
        z_out[k] = total.astype(BF16)
        for d in range(1, NZ):
            z_copy(k, d).start()
        z_own[k] = part[k, yhi, z, core]

    def stage_z(k):
        flows = z_own[k]
        for d in range(1, NZ):
            z_copy(k, d).wait_recv()
            flows = flows + z_in[k, d - 1].astype(F32)
        lim = limits[...]
        penalty, adjoint = epilogue(flows, jnp.concatenate([lim] * NYL, axis=1))
        adj[k, yhi, z, core] = adjoint.astype(BF16)
        for d in range(1, NZ):
            gz_copy(k, d).start()
        for b in range(NYL):
            pen_v[k, b] = penalty[:, b * LANES : (b + 1) * LANES]
            pen_copy(k, b).start()

    def pen_copy(k, b):
        return pltpu.make_async_copy(pen_v.at[k, b], penalty_out.at[:, columns(k, b)], pen_sem.at[k, b])

    def stage_gather_z(k):
        for d in range(1, NZ):
            gz_arrival(k, d).wait_recv()
        gy_copy(k, yhi).start()
        gc_copy(k, True, core).start()

    def stage_gather_y(k):
        gy_copy(k, 1 - yhi).wait_recv()
        gc_copy(k, False, core).start()

    def transpose_some(first, count):
        strip = 256

        def body(i, _):
            s = pl.ds(pl.multiple_of(i * strip, strip), strip)
            pt_v[s] = p_v[:, s].T
            return 0

        lax.fori_loop(first, first + count, body, 0)

    def product(k, row0):
        lhs = pt_v[pl.ds(pl.multiple_of(row0, tile), tile)]
        rhs = adj[k].reshape(rows, width)
        return jnp.dot(lhs, rhs, preferred_element_type=F32)

    def opp_copy(side, j):
        return remote(
            opp_out.at[side, j], opp_in.at[side, j], opp_sem.at[0, side, j], opp_sem.at[1, side, j], (right, left)[side]
        )

    def right_copy(i):
        return remote(right_out.at[i], right_in.at[i], right_sem.at[0, i], right_sem.at[1, i], right)

    def left_copy(i):
        return remote(left_out.at[i], left_in.at[i], left_sem.at[0, i], left_sem.at[1, i], left)

    def stage_block(k):
        gc_copy(k, True, 1 - core).wait_recv()
        gc_copy(k, False, 1 - core).wait_recv()

        def opposite(j, _):
            opp_out[0, j] = product(0, j * tile).astype(BF16)
            opp_copy(0, j).start()
            opp_out[1, j] = product(0, half + j * tile).astype(BF16)
            opp_copy(1, j).start()
            return 0

        def rightward(j, _):
            right_out[steps + j] = product(1, half + j * tile).astype(BF16)
            right_copy(steps + j).start()
            return 0

        def leftward(j, _):
            left_out[j] = product(2, j * tile).astype(BF16)
            left_copy(j).start()
            return 0

        if k < 3:
            lax.fori_loop(0, steps, (opposite, rightward, leftward)[k], 0)

    stages = [stage_matmul, stage_core, stage_y, stage_z, stage_gather_z, stage_gather_y, stage_block]
    strips = buses // 256
    for t in range(NX + len(stages) - 1):
        for s in reversed(range(len(stages))):
            if 0 <= t - s < NX:
                stages[s](t - s)
        if 1 <= t <= 4:
            transpose_some((t - 1) * strips // 4, strips // 4)

    def relay(j, _):
        mine = product(1, j * tile)
        opp_copy(0, j).wait_recv()
        right_out[j] = (mine + opp_in[0, j].astype(F32)).astype(BF16)
        right_copy(j).start()
        mine = product(2, half + j * tile)
        opp_copy(1, j).wait_recv()
        left_out[steps + j] = (mine + opp_in[1, j].astype(F32)).astype(BF16)
        left_copy(steps + j).start()
        return 0

    lax.fori_loop(0, steps, relay, 0)

    def pair_copy(i):
        return remote(pair_out.at[i], pair_in.at[i], pair_sem.at[0, i], pair_sem.at[1, i], pair)

    def sens_copy(i):
        return pltpu.make_async_copy(
            sens_v.at[i], sens_out.at[pl.ds(pl.multiple_of(i * tile, tile), tile)], sens_sem.at[i]
        )

    def reduce_x(i):
        total = product(3, i * tile)
        right_copy(i).wait_recv()
        left_copy(i).wait_recv()
        total = total + right_in[i].astype(F32) + left_in[i].astype(F32)
        first, second = total[:, :LANES], total[:, LANES:]
        low = ylo == 0
        pair_own[i] = jnp.where(low, first, second)
        pair_out[i] = jnp.where(low, second, first).astype(BF16)
        pair_copy(i).start()

    def finish(i):
        pair_copy(i).wait_recv()
        sens_v[i] = pair_own[i] + pair_in[i].astype(F32)
        sens_copy(i).start()

    def last(j, _):
        @pl.when(j < steps)
        def _():
            reduce_x(j)
            reduce_x(steps + j)

        @pl.when(j > 0)
        def _():
            finish(j - 1)
            finish(steps + j - 1)

        return 0

    lax.fori_loop(0, steps + 1, last, 0)

    for k in range(NX):
        core_copy(k).wait_send()
        y_copy(k).wait_send()
        gy_copy(k, yhi).wait_send()
        gc_copy(k, True, core).wait_send()
        gc_copy(k, False, core).wait_send()
        for d in range(1, NZ):
            z_copy(k, d).wait_send()
            gz_copy(k, d).wait_send()
        for b in range(NYL):
            pen_copy(k, b).wait()

    def drain(j, _):
        for side in range(2):
            opp_copy(side, j).wait_send()
            i = side * steps + j
            right_copy(i).wait_send()
            left_copy(i).wait_send()
            pair_copy(i).wait_send()
            sens_copy(i).wait()
        return 0

    lax.fori_loop(0, steps, drain, 0)


def local(ptdf, load_codes, limit_codes):
    rows, buses = ptdf.shape
    hours = load_codes.shape[1]
    own = rows // (NYH * NZ * NC)
    width = NYL * LANES
    tile = 128
    steps = buses // 2 // tile
    offset = lax.axis_index("bus") * own
    limits = lax.dynamic_slice_in_dim(limit_codes, offset, own, 0).astype(F32) / 64.0
    limits = jnp.broadcast_to(limits[:, None], (own, LANES))
    dma = pltpu.SemaphoreType.DMA
    scratch = [
        pltpu.VMEM((rows, buses), BF16),
        pltpu.VMEM((buses, rows), BF16),
        pltpu.VMEM((NX, NYL, buses, LANES), jnp.int32),
        pltpu.VMEM((buses, width), BF16),
        pltpu.VMEM((NX, NYH, NZ, NC, own, width), F32),
        pltpu.VMEM((NX, NYH, NZ, own, width), F32),
        pltpu.VMEM((NX, NZ, own, width), BF16),
        pltpu.VMEM((NX, NZ, own, width), BF16),
        pltpu.VMEM((NX, NZ, own, width), BF16),
        pltpu.VMEM((NX, NZ - 1, own, width), BF16),
        pltpu.VMEM((NX, own, width), F32),
        pltpu.VMEM((NX, NYH, NZ, NC, own, width), BF16),
        pltpu.VMEM((NX, NYL, own, LANES), F32),
        pltpu.VMEM((2, steps, tile, width), BF16),
        pltpu.VMEM((2, steps, tile, width), BF16),
        pltpu.VMEM((2 * steps, tile, width), BF16),
        pltpu.VMEM((2 * steps, tile, width), BF16),
        pltpu.VMEM((2 * steps, tile, width), BF16),
        pltpu.VMEM((2 * steps, tile, width), BF16),
        pltpu.VMEM((2 * steps, tile, LANES), F32),
        pltpu.VMEM((2 * steps, tile, LANES), BF16),
        pltpu.VMEM((2 * steps, tile, LANES), BF16),
        pltpu.VMEM((2 * steps, tile, LANES), F32),
        dma((4,)),
        dma((NX, NYL)),
        dma((2, NX)),
        dma((2, NX)),
        dma((NX, NZ - 1)),
        dma((NX, NZ - 1)),
        dma((NX, NZ - 1)),
        dma((NX, NZ - 1)),
        dma((2, NX)),
        dma((2, NX, 2)),
        dma((2, 2, steps)),
        dma((2, 2 * steps)),
        dma((2, 2 * steps)),
        dma((2, 2 * steps)),
        dma((NX, NYL)),
        dma((2 * steps,)),
    ]
    anywhere = pl.BlockSpec(memory_space=pl.ANY)
    return pl.pallas_call(
        kernel,
        out_shape=(
            jax.ShapeDtypeStruct((own, hours), F32),
            jax.ShapeDtypeStruct((buses, LANES), F32),
        ),
        in_specs=[anywhere, anywhere, pl.BlockSpec(memory_space=pltpu.VMEM)],
        out_specs=(anywhere, anywhere),
        scratch_shapes=scratch,
        compiler_params=pltpu.CompilerParams(
            collective_id=0, has_side_effects=True, vmem_limit_bytes=48 * 1024 * 1024
        ),
    )(ptdf, load_codes, limits)


def solution(mesh):
    return jax.shard_map(
        local,
        mesh=mesh,
        in_specs=(P("br", "bus"), P("bus", None), P("br")),
        out_specs=(P(("br", "bus"), None), P("bus", "br")),
        check_vma=False,
    )
```

time: 417 us -> 94.6 us (0.23)
  waiting for transfers between devices: 368 us -> 0 us
  Pallas kernels: 0 us -> 87.5 us
  matrix products: 24.4 us -> 0 us
  between operations: 14.1 us -> 0.64 us
    psum x1 -> x0, waiting for transfers between devices: 280 us -> none  [local(): flows = lax.psum(partial_flows, 'bus')]
    reduce_scatter x1 -> x0, waiting for transfers between devices: 88.7 us -> none  [local(): lax.psum_scatter(partial_sens, 'br', scatter_dimension=1, tiled=True)]
    pallas_call x0 -> x1, Pallas kernels: none -> 87.5 us  [local(): pl.pallas_call(kernel, out_shape=(jax.ShapeDtypeStruct((own, hours), F32)...]
    dot_general x2 -> x0, matrix products: 24.4 us -> none  [the longest x1 13.3 us: local(): lax.dot_general(ptdf, adjoint_block, (((0,), (0,)), ((), ())), preferred_...]
  transfers between devices with their start and end apart: 2 -> 0, of which waited for: 2 -> 0; matrix products, arithmetic and copies ran while one was open for 1% -> 0% of each run, Pallas kernels for 0% -> 0%
where the time goes in v2:
time: 94.6 us; the launch traced here: 92.8 us
  Pallas kernels  87.5 us (92%)
  local copies, waits for them, and re-layouts  3.89 us (4%)
    pallas_call x1, Pallas kernels, local(): pl.pallas_call(kernel, out_shape=(jax.ShapeDtypeStruct((own, hours), F32)...  87.5 us
    unnamed x4, local copies, waits for them, and re-layouts  3.82 us

profile of v2, /device:TPU:8, one launch (start us, length us, event | category | flops | bytes accessed | tf_op | source)
XLA Modules:
  0.0 92.8 jit_solution(3337551297001158780)
XLA Ops:
  0.6 0.8 convert_multiply_fusion
  1.4 0.1 broadcast_in_dim.2.limits
  1.5 0.0 copy-start
  1.5 2.2 %copy-done = bf16[1024,2048]{1,0:T(8,128)(2,1)S(1)} copy-done((bf16[1024,2048]{1,0:T(8,128)(2,1)S(1)}, bf16[1024,2048]{1,0:T(8,128)(2,1)}, u32[]{:S(2)}) %copy-start) | copy-done | bytes 4194328
  3.7 87.5 %shard_map.50 = (f32[32,1024]{1,0:T(8,128)S(1)}, f32[2048,128]{1,0:T(8,128)S(1)}) custom-call(bf16[1024,2048]{1,0:T(8,128)(2,1)S(1)} %copy-done, s32[2048,1024]{1,0:T(8,128)} %codes.1, f32[32,128]{1,0:T(8,128)S(1)} %broadcast_in_dim.2.limits), custom_call_target="tpu_custom_call" | custom-call | tf_op jit(solution)/shard_map/pallas_call | solution.py:370
  91.2 0.7 copy.7
  91.8 1.0 %copy.8 = f32[2048,128]{1,0:T(8,128)} copy(f32[2048,128]{1,0:T(8,128)S(1)} %get-tuple-element.5) | data formatting | bytes 2097152
Async XLA Ops:
  1.5 2.2 %copy-start = (bf16[1024,2048]{1,0:T(8,128)(2,1)S(1)}, bf16[1024,2048]{1,0:T(8,128)(2,1)}, u32[]{:S(2)}) copy-start(bf16[1024,2048]{1,0:T(8,128)(2,1)} %ptdf.1) | copy-start | bytes 12582916

commit v3 on v0

v3 whole, which is shorter than its diff:
```python
import jax
import jax.numpy as jnp
from jax import lax
from jax.experimental import pallas as pl
from jax.experimental.pallas import tpu as pltpu
from jax.sharding import PartitionSpec as P

MESH = pl.DeviceIdType.MESH
NX, NYL, NYH, NZ, NC = 4, 2, 2, 8, 2
LANES = 128
UNITS = 8
ORDER = (0, 1, 2, 4, 6, 3, 5, 7)
LAGS = (1, 3, 5, 7, 9, 10)
MATMULS = (0, 1, 2, 4)
RELAY_DELAY = (0, 0)
PAIR_DELAY = 2
F32, BF16 = jnp.float32, jnp.bfloat16


def epilogue(flows, limits):
    magnitude = jnp.sqrt(flows * flows + 1.0)
    zvalue = 4.0 * (magnitude / limits - 1.0)
    decay = jnp.exp(-jnp.abs(zvalue))
    penalty = (jnp.maximum(zvalue, 0.0) + jnp.log1p(decay)) * 0.25
    sigmoid = jnp.where(zvalue >= 0.0, 1.0, decay) / (1.0 + decay)
    adjoint = sigmoid * flows / (magnitude * limits)
    return penalty, adjoint


def kernel(
    ptdf, codes, limit_codes, penalty_out, sens_out,
    p_v, codes_v, inj_v, limit_s, limits, part, core_in, y_out, y_in, z_out, z_in, z_own, adj, pen_v, s_v,
    opp_out, opp_in, right_out, left_out, right_in, left_in, pair_out, pair_in, sens_v,
    p_sem, c_sem, l_sem, core_sem, y_sem, zs_sem, zr_sem, gzs_sem, gzr_sem, gy_sem, gc_sem,
    opp_sem, right_sem, left_sem, pair_sem, pen_sem, sens_sem,
):
    br, bus = lax.axis_index("br"), lax.axis_index("bus")
    x, ylo = lax.rem(br, NX), br // NX
    core, z, yhi = lax.rem(bus, NC), lax.rem(bus // NC, NZ), bus // (NC * NZ)
    rows, buses = p_v.shape
    own = rows // (NYH * NZ * NC)
    steps, tile = opp_out.shape[2], opp_out.shape[3]
    half = steps * tile

    def at_bus(h, zz, c):
        return (br, (h * NZ + zz) * NC + c)

    sibling = at_bus(yhi, z, 1 - core)
    far_y = at_bus(1 - yhi, z, core)

    def z_peer(d):
        return at_bus(yhi, lax.rem(z + d, NZ), core)

    right = (ylo * NX + lax.rem(x + 1, NX), bus)
    left = (ylo * NX + lax.rem(x + NX - 1, NX), bus)
    pair = ((1 - ylo) * NX + x, bus)
    partners = [sibling, far_y, right, left, pair] + [z_peer(d) for d in range(1, NZ)]

    def columns(u):
        k, s = u // 2, lax.rem(u, 2)
        ahead = jnp.where(k == 0, 2, jnp.where(k == 1, 1, jnp.where(k == 2, 3, 0)))
        block = lax.rem(x + ahead, NX) + NX * jnp.where(s == 0, 1 - ylo, ylo)
        return pl.ds(pl.multiple_of(block * LANES, LANES), LANES)

    def pick(index, choices):
        value = jnp.int32(choices[-1])
        for i, choice in enumerate(choices[:-1]):
            value = jnp.where(index == i, choice, value)
        return value

    def remote(src, dst, send, recv, device):
        return pltpu.make_async_remote_copy(
            src_ref=src, dst_ref=dst, send_sem=send, recv_sem=recv, device_id=device, device_id_type=MESH
        )

    def codes_copy(u):
        return pltpu.make_async_copy(codes.at[:, columns(u)], codes_v.at[u], c_sem.at[u])

    p_copy = pltpu.make_async_copy(ptdf, p_v, p_sem)
    limit_copy = pltpu.make_async_copy(limit_codes, limit_s, l_sem)
    codes_copy(jnp.int32(0)).start()
    codes_copy(jnp.int32(1)).start()
    p_copy.start()
    limit_copy.start()
    barrier = pltpu.get_barrier_semaphore()
    for device in partners:
        pl.semaphore_signal(barrier, inc=1, device_id=device, device_id_type=MESH)
    pl.semaphore_wait(barrier, len(partners))

    def core_copy(u):
        return remote(part.at[u, :, :, 1 - core], core_in.at[u], core_sem.at[0, u], core_sem.at[1, u], sibling)

    def y_copy(u):
        return remote(y_out.at[u], y_in.at[u], y_sem.at[0, u], y_sem.at[1, u], far_y)

    def z_copy(u, d):
        return remote(
            z_out.at[u, lax.rem(z + d, NZ)], z_in.at[u, d - 1], zs_sem.at[u, d - 1], zr_sem.at[u, d - 1], z_peer(d)
        )

    def gz_copy(u, d):
        mine = adj.at[u, yhi, z, core]
        return remote(mine, mine, gzs_sem.at[u, d - 1], gzr_sem.at[u, d - 1], z_peer(d))

    def gz_arrival(u, d):
        theirs = adj.at[u, yhi, lax.rem(z + NZ - d, NZ), core]
        return remote(theirs, theirs, gzs_sem.at[u, d - 1], gzr_sem.at[u, d - 1], z_peer(d))

    def gy_copy(u, h):
        rows_of = adj.at[u, h, :, core]
        return remote(rows_of, rows_of, gy_sem.at[0, u], gy_sem.at[1, u], far_y)

    def gc_copy(u, near, c):
        rows_of = adj.at[u, yhi if near else 1 - yhi, :, c]
        which = 0 if near else 1
        return remote(rows_of, rows_of, gc_sem.at[0, u, which], gc_sem.at[1, u, which], sibling)

    def pen_copy(u):
        return pltpu.make_async_copy(pen_v.at[u], penalty_out.at[:, columns(u)], pen_sem.at[u])

    def stage_matmul(k):
        strip = 256
        for s in range(2):
            codes_copy(2 * k + s).wait()

        def convert(i, _):
            at = pl.ds(pl.multiple_of(i * strip, strip), strip)
            for s in range(2):
                values = codes_v[2 * k + s, at].astype(F32) * (1.0 / 1024.0)
                inj_v[at, s * LANES : (s + 1) * LANES] = values.astype(BF16)
            return 0

        lax.fori_loop(0, buses // strip, convert, 0)
        @pl.when(k == 0)
        def _():
            p_copy.wait()
            for u in range(2, UNITS):
                codes_copy(jnp.int32(u)).start()

        product = jnp.dot(p_v[...], inj_v[...], preferred_element_type=F32)
        for s in range(2):
            part[2 * k + s] = product[:, s * LANES : (s + 1) * LANES].reshape(NYH, NZ, NC, own, LANES)

        for s in range(2):
            core_copy(2 * k + s).start()

        @pl.when(k == 0)
        def _():
            limit_copy.wait()
            row = lax.broadcasted_iota(jnp.int32, (own, LANES), 0)
            values = jnp.zeros((own, LANES), F32)
            for i in range(own):
                values = jnp.where(row == i, limit_s[bus * own + i].astype(F32), values)
            limits[...] = values * (1.0 / 64.0)

    def stage_core(u):
        core_copy(u).wait_recv()
        y_out[u] = (part[u, 1 - yhi, :, core] + core_in[u, 1 - yhi]).astype(BF16)
        y_copy(u).start()

    def stage_y(u):
        y_copy(u).wait_recv()
        total = part[u, yhi, :, core] + core_in[u, yhi] + y_in[u].astype(F32)
        part[u, yhi, :, core] = total
        z_out[u] = total.astype(BF16)
        for d in range(1, NZ):
            z_copy(u, d).start()
        z_own[u] = part[u, yhi, z, core]

    def stage_z(u):
        flows = z_own[u]
        for d in range(1, NZ):
            z_copy(u, d).wait_recv()
            flows = flows + z_in[u, d - 1].astype(F32)
        penalty, adjoint = epilogue(flows, limits[...])
        adj[u, yhi, z, core] = adjoint.astype(BF16)
        for d in range(1, NZ):
            gz_copy(u, d).start()
        pen_v[u] = penalty
        pen_copy(u).start()

    def stage_gather_z(u):
        for d in range(1, NZ):
            gz_arrival(u, d).wait_recv()
        gy_copy(u, yhi).start()
        gc_copy(u, True, core).start()

    def stage_gather_y(u):
        gy_copy(u, 1 - yhi).wait_recv()
        gc_copy(u, False, core).start()

    def opp_copy(s, side, j):
        return remote(
            opp_out.at[s, side, j], opp_in.at[s, side, j], opp_sem.at[0, s, side, j], opp_sem.at[1, s, side, j],
            (right, left)[side],
        )

    def right_copy(s, i):
        return remote(right_out.at[s, i], right_in.at[s, i], right_sem.at[0, s, i], right_sem.at[1, s, i], right)

    def left_copy(s, i):
        return remote(left_out.at[s, i], left_in.at[s, i], left_sem.at[0, s, i], left_sem.at[1, s, i], left)

    def tile_at(i):
        return pl.ds(pl.multiple_of(i * tile, tile), tile)

    def stage_sens(u):
        gc_copy(u, True, 1 - core).wait_recv()
        gc_copy(u, False, 1 - core).wait_recv()
        k, s = u // 2, lax.rem(u, 2)
        rhs = adj[u].reshape(rows, LANES)
        s_v[u] = lax.dot_general(p_v[...], rhs, (((0,), (0,)), ((), ())), preferred_element_type=F32)

        def opposite(j, _):
            opp_out[s, 0, j] = s_v[u, tile_at(j)].astype(BF16)
            opp_copy(s, 0, j).start()
            opp_out[s, 1, j] = s_v[u, tile_at(steps + j)].astype(BF16)
            opp_copy(s, 1, j).start()
            return 0

        def rightward(j, _):
            right_out[s, steps + j] = s_v[u, tile_at(steps + j)].astype(BF16)
            right_copy(s, steps + j).start()
            return 0

        def leftward(j, _):
            left_out[s, j] = s_v[u, tile_at(j)].astype(BF16)
            left_copy(s, j).start()
            return 0

        for kind, send in enumerate((opposite, rightward, leftward)):

            @pl.when(k == kind)
            def _(send=send):
                lax.fori_loop(0, steps, send, 0)

    def relay(s):
        def body(j, _):
            opp_copy(s, 0, j).wait_recv()
            right_out[s, j] = (s_v[2 + s, tile_at(j)] + opp_in[s, 0, j].astype(F32)).astype(BF16)
            right_copy(s, j).start()
            opp_copy(s, 1, j).wait_recv()
            left_out[s, steps + j] = (s_v[4 + s, tile_at(steps + j)] + opp_in[s, 1, j].astype(F32)).astype(BF16)
            left_copy(s, steps + j).start()
            return 0

        lax.fori_loop(0, steps, body, 0)

    stages = [stage_core, stage_y, stage_z, stage_gather_z, stage_gather_y, stage_sens]
    def pair_copy(i):
        return remote(pair_out.at[i], pair_in.at[i], pair_sem.at[0, i], pair_sem.at[1, i], pair)

    def sens_copy(i):
        return pltpu.make_async_copy(sens_v.at[i], sens_out.at[tile_at(i)], sens_sem.at[i])

    def x_sum(s, i):
        right_copy(s, i).wait_recv()
        left_copy(s, i).wait_recv()
        return s_v[6 + s, tile_at(i)] + right_in[s, i].astype(F32) + left_in[s, i].astype(F32)

    def for_pair(j, _):
        for i in (j, steps + j):
            pair_out[i] = x_sum(0, i).astype(BF16)
            pair_copy(i).start()
        return 0

    def for_self(j, _):
        for i in (j, steps + j):
            total = x_sum(1, i)
            pair_copy(i).wait_recv()
            sens_v[i] = total + pair_in[i].astype(F32)
            sens_copy(i).start()
        return 0

    waits = {unit: ORDER.index(unit) + LAGS[-1] for unit in range(UNITS)}
    relay_at = [max(waits[2 + s], waits[4 + s]) + RELAY_DELAY[s] for s in range(2)]
    pair_at = max(relay_at[0], waits[6]) + PAIR_DELAY

    def run(t, _):
        for lag, stage in reversed(list(zip(LAGS, stages))):
            p = t - lag

            @pl.when((p >= 0) & (p < UNITS))
            def _(p=p, stage=stage):
                stage(pick(p, ORDER))

        this = sum(jnp.where(t == at, k, 0) for k, at in enumerate(MATMULS))

        @pl.when((this > 0) | (t == MATMULS[0]))
        def _():
            stage_matmul(this)

        @pl.when((t == relay_at[0]) | (t == relay_at[1]))
        def _():
            relay(jnp.where(t == relay_at[0], 0, 1))

        @pl.when(t == pair_at)
        def _():
            lax.fori_loop(0, steps, for_pair, 0)

        return 0

    lax.fori_loop(0, max(UNITS + LAGS[-1], relay_at[1] + 1, pair_at + 1), run, 0)
    lax.fori_loop(0, steps, for_self, 0)

    def drain_unit(u, _):
        core_copy(u).wait_send()
        y_copy(u).wait_send()
        gy_copy(u, yhi).wait_send()
        gc_copy(u, True, core).wait_send()
        gc_copy(u, False, core).wait_send()
        for d in range(1, NZ):
            z_copy(u, d).wait_send()
            gz_copy(u, d).wait_send()
        pen_copy(u).wait()
        return 0

    lax.fori_loop(0, UNITS, drain_unit, 0)

    def drain(j, _):
        for side in range(2):
            i = side * steps + j
            for s in range(2):
                opp_copy(s, side, j).wait_send()
                right_copy(s, i).wait_send()
                left_copy(s, i).wait_send()
            pair_copy(i).wait_send()
            sens_copy(i).wait()
        return 0

    lax.fori_loop(0, steps, drain, 0)


def local(ptdf, load_codes, limit_codes):
    rows, buses = ptdf.shape
    hours = load_codes.shape[1]
    own = rows // (NYH * NZ * NC)
    tile = 256
    steps = buses // 2 // tile
    dma = pltpu.SemaphoreType.DMA
    piece = (UNITS, NZ, own, LANES)
    tiles = (2, 2 * steps, tile, LANES)
    scratch = [
        pltpu.VMEM((rows, buses), BF16),
        pltpu.VMEM((UNITS, buses, LANES), jnp.int32),
        pltpu.VMEM((buses, 2 * LANES), BF16),
        pltpu.SMEM((rows,), jnp.int32),
        pltpu.VMEM((own, LANES), F32),
        pltpu.VMEM((UNITS, NYH, NZ, NC, own, LANES), F32),
        pltpu.VMEM((UNITS, NYH, NZ, own, LANES), F32),
        pltpu.VMEM(piece, BF16),
        pltpu.VMEM(piece, BF16),
        pltpu.VMEM(piece, BF16),
        pltpu.VMEM((UNITS, NZ - 1, own, LANES), BF16),
        pltpu.VMEM((UNITS, own, LANES), F32),
        pltpu.VMEM((UNITS, NYH, NZ, NC, own, LANES), BF16),
        pltpu.VMEM((UNITS, own, LANES), F32),
        pltpu.VMEM((UNITS, buses, LANES), F32),
        pltpu.VMEM((2, 2, steps, tile, LANES), BF16),
        pltpu.VMEM((2, 2, steps, tile, LANES), BF16),
        pltpu.VMEM(tiles, BF16),
        pltpu.VMEM(tiles, BF16),
        pltpu.VMEM(tiles, BF16),
        pltpu.VMEM(tiles, BF16),
        pltpu.VMEM(tiles[1:], BF16),
        pltpu.VMEM(tiles[1:], BF16),
        pltpu.VMEM(tiles[1:], F32),
        dma,
        dma((UNITS,)),
        dma,
        dma((2, UNITS)),
        dma((2, UNITS)),
        dma((UNITS, NZ - 1)),
        dma((UNITS, NZ - 1)),
        dma((UNITS, NZ - 1)),
        dma((UNITS, NZ - 1)),
        dma((2, UNITS)),
        dma((2, UNITS, 2)),
        dma((2, 2, 2, steps)),
        dma((2, 2, 2 * steps)),
        dma((2, 2, 2 * steps)),
        dma((2, 2 * steps)),
        dma((UNITS,)),
        dma((2 * steps,)),
    ]
    anywhere = pl.BlockSpec(memory_space=pl.ANY)
    return pl.pallas_call(
        kernel,
        out_shape=(
            jax.ShapeDtypeStruct((own, hours), F32),
            jax.ShapeDtypeStruct((buses, LANES), F32),
        ),
        in_specs=[anywhere] * 3,
        out_specs=(anywhere, anywhere),
        scratch_shapes=scratch,
        compiler_params=pltpu.CompilerParams(
            collective_id=0, has_side_effects=True, vmem_limit_bytes=42 * 1024 * 1024
        ),
    )(ptdf, load_codes, limit_codes)


def solution(mesh):
    return jax.shard_map(
        local,
        mesh=mesh,
        in_specs=(P("br", "bus"), P("bus", None), P("br")),
        out_specs=(P(("br", "bus"), None), P("bus", "br")),
        check_vma=False,
    )
```

time: 417 us -> 80.9 us (0.19)
  waiting for transfers between devices: 368 us -> 0 us
  Pallas kernels: 0 us -> 74.2 us
  matrix products: 24.4 us -> 0 us
  between operations: 14.1 us -> 0.65 us
  other arithmetic: 4.33 us -> 0 us
    psum x1 -> x0, waiting for transfers between devices: 280 us -> none  [local(): flows = lax.psum(partial_flows, 'bus')]
    reduce_scatter x1 -> x0, waiting for transfers between devices: 88.7 us -> none  [local(): lax.psum_scatter(partial_sens, 'br', scatter_dimension=1, tiled=True)]
    pallas_call x0 -> x1, Pallas kernels: none -> 74.2 us  [local(): pl.pallas_call(kernel, out_shape=(jax.ShapeDtypeStruct((own, hours), F32)...]
    dot_general x2 -> x0, matrix products: 24.4 us -> none  [the longest x1 13.3 us: local(): lax.dot_general(ptdf, adjoint_block, (((0,), (0,)), ((), ())), preferred_...]
  transfers between devices with their start and end apart: 2 -> 0, of which waited for: 2 -> 0; matrix products, arithmetic and copies ran while one was open for 1% -> 0% of each run, Pallas kernels for 0% -> 0%
where the time goes in v3:
time: 80.9 us; the launch traced here: 79.3 us
  Pallas kernels  74.2 us (92%)
  local copies, waits for them, and re-layouts  4.49 us (6%)
    pallas_call x1, Pallas kernels, local(): pl.pallas_call(kernel, out_shape=(jax.ShapeDtypeStruct((own, hours), F32)...  74.2 us
    unnamed x6, local copies, waits for them, and re-layouts  4.49 us

profile of v3, /device:TPU:8, one launch (start us, length us, event | category | flops | bytes accessed | tf_op | source)
XLA Modules:
  0.0 79.3 jit_solution(17529445962652980968)
XLA Ops:
  0.6 0.0 copy-start
  0.6 2.2 %copy-done = bf16[1024,2048]{1,0:T(8,128)(2,1)S(1)} copy-done((bf16[1024,2048]{1,0:T(8,128)(2,1)S(1)}, bf16[1024,2048]{1,0:T(8,128)(2,1)}, u32[]{:S(2)}) %copy-start) | copy-done | bytes 4194328
  2.8 0.0 copy-start.1
  2.8 0.7 copy-done.1
  3.5 74.2 %shard_map.50 = (f32[32,1024]{1,0:T(8,128)S(1)}, f32[2048,128]{1,0:T(8,128)S(1)}) custom-call(bf16[1024,2048]{1,0:T(8,128)(2,1)S(1)} %copy-done, s32[2048,1024]{1,0:T(8,128)} %codes.1, s32[1024]{0:T(1024)S(1)} %copy-done.1), custom_call_target="tpu_custom_call" | custom-call | tf_op jit(solution)/shard_map/pallas_call | solution.py:387
  77.7 0.7 copy.7
  78.4 1.0 %copy.8 = f32[2048,128]{1,0:T(8,128)} copy(f32[2048,128]{1,0:T(8,128)S(1)} %get-tuple-element.5) | data formatting | bytes 2097152
Async XLA Ops:
  0.6 2.2 %copy-start = (bf16[1024,2048]{1,0:T(8,128)(2,1)S(1)}, bf16[1024,2048]{1,0:T(8,128)(2,1)}, u32[]{:S(2)}) copy-start(bf16[1024,2048]{1,0:T(8,128)(2,1)} %ptdf.1) | copy-start | bytes 12582916
  2.8 0.7 copy-start.1

commit v4 on v3

--- a/solution.py
+++ b/solution.py
@@ -48,13 +48,11 @@
     sibling = at_bus(yhi, z, 1 - core)
     far_y = at_bus(1 - yhi, z, core)
 
-    def z_peer(d):
-        return at_bus(yhi, lax.rem(z + d, NZ), core)
-
+    z_peers = [at_bus(yhi, lax.rem(z + d, NZ), core) for d in range(NZ)]
     right = (ylo * NX + lax.rem(x + 1, NX), bus)
     left = (ylo * NX + lax.rem(x + NX - 1, NX), bus)
     pair = ((1 - ylo) * NX + x, bus)
-    partners = [sibling, far_y, right, left, pair] + [z_peer(d) for d in range(1, NZ)]
+    partners = [sibling, far_y, right, left, pair] + z_peers[1:]
 
     def columns(u):
         k, s = u // 2, lax.rem(u, 2)
@@ -95,16 +93,15 @@
 
     def z_copy(u, d):
         return remote(
-            z_out.at[u, lax.rem(z + d, NZ)], z_in.at[u, d - 1], zs_sem.at[u, d - 1], zr_sem.at[u, d - 1], z_peer(d)
+            z_out.at[u, lax.rem(z + d, NZ)], z_in.at[u, d - 1], zs_sem.at[u], zr_sem.at[u], z_peers[d]
         )
 
     def gz_copy(u, d):
         mine = adj.at[u, yhi, z, core]
-        return remote(mine, mine, gzs_sem.at[u, d - 1], gzr_sem.at[u, d - 1], z_peer(d))
-
-    def gz_arrival(u, d):
-        theirs = adj.at[u, yhi, lax.rem(z + NZ - d, NZ), core]
-        return remote(theirs, theirs, gzs_sem.at[u, d - 1], gzr_sem.at[u, d - 1], z_peer(d))
+        return remote(mine, mine, gzs_sem.at[u], gzr_sem.at[u], z_peers[d])
+
+    def all_z(u, send, recv):
+        return remote(z_in.at[u], z_in.at[u], send.at[u], recv.at[u], z_peers[1])
 
     def gy_copy(u, h):
         rows_of = adj.at[u, h, :, core]
@@ -163,25 +160,24 @@
         total = part[u, yhi, :, core] + core_in[u, yhi] + y_in[u].astype(F32)
         part[u, yhi, :, core] = total
         z_out[u] = total.astype(BF16)
-        for d in range(1, NZ):
+        for d in (4, 3, 5, 2, 6, 1, 7):
             z_copy(u, d).start()
         z_own[u] = part[u, yhi, z, core]
 
     def stage_z(u):
         flows = z_own[u]
+        all_z(u, zs_sem, zr_sem).wait_recv()
         for d in range(1, NZ):
-            z_copy(u, d).wait_recv()
             flows = flows + z_in[u, d - 1].astype(F32)
         penalty, adjoint = epilogue(flows, limits[...])
         adj[u, yhi, z, core] = adjoint.astype(BF16)
-        for d in range(1, NZ):
+        for d in (4, 3, 5, 2, 6, 1, 7):
             gz_copy(u, d).start()
         pen_v[u] = penalty
         pen_copy(u).start()
 
     def stage_gather_z(u):
-        for d in range(1, NZ):
-            gz_arrival(u, d).wait_recv()
+        all_z(u, gzs_sem, gzr_sem).wait_recv()
         gy_copy(u, yhi).start()
         gc_copy(u, True, core).start()
 
@@ -309,9 +305,8 @@
         gy_copy(u, yhi).wait_send()
         gc_copy(u, True, core).wait_send()
         gc_copy(u, False, core).wait_send()
-        for d in range(1, NZ):
-            z_copy(u, d).wait_send()
-            gz_copy(u, d).wait_send()
+        all_z(u, zs_sem, zr_sem).wait_send()
+        all_z(u, gzs_sem, gzr_sem).wait_send()
         pen_copy(u).wait()
         return 0
 
@@ -335,7 +330,7 @@
     rows, buses = ptdf.shape
     hours = load_codes.shape[1]
     own = rows // (NYH * NZ * NC)
-    tile = 256
+    tile = 512
     steps = buses // 2 // tile
     dma = pltpu.SemaphoreType.DMA
     piece = (UNITS, NZ, own, LANES)
@@ -370,10 +365,10 @@
         dma,
         dma((2, UNITS)),
         dma((2, UNITS)),
-        dma((UNITS, NZ - 1)),
-        dma((UNITS, NZ - 1)),
-        dma((UNITS, NZ - 1)),
-        dma((UNITS, NZ - 1)),
+        dma((UNITS,)),
+        dma((UNITS,)),
+        dma((UNITS,)),
+        dma((UNITS,)),
         dma((2, UNITS)),
         dma((2, UNITS, 2)),
         dma((2, 2, 2, steps)),

time: 80.9 us -> 77 us (0.952)
  Pallas kernels: 74.2 us -> 70.7 us
    pallas_call x1, Pallas kernels: 74.2 us -> 70.7 us  [local(): pl.pallas_call(kernel, out_shape=(jax.ShapeDtypeStruct((own, hours), F32)...]
where the time goes in v4:
time: 77 us; the launch traced here: 75.9 us
  Pallas kernels  70.7 us (92%)
  local copies, waits for them, and re-layouts  4.49 us (6%)
    pallas_call x1, Pallas kernels, local(): pl.pallas_call(kernel, out_shape=(jax.ShapeDtypeStruct((own, hours), F32)...  70.7 us
    unnamed x6, local copies, waits for them, and re-layouts  4.49 us

profile of v4, /device:TPU:8, one launch (start us, length us, event | category | flops | bytes accessed | tf_op | source)
XLA Modules:
  0.0 75.9 jit_solution(8146840702334286229)
XLA Ops:
  0.6 0.0 copy-start
  0.6 2.2 %copy-done = bf16[1024,2048]{1,0:T(8,128)(2,1)S(1)} copy-done((bf16[1024,2048]{1,0:T(8,128)(2,1)S(1)}, bf16[1024,2048]{1,0:T(8,128)(2,1)}, u32[]{:S(2)}) %copy-start) | copy-done | bytes 4194328
  2.8 0.0 copy-start.1
  2.8 0.7 copy-done.1
  3.5 70.7 %shard_map.50 = (f32[32,1024]{1,0:T(8,128)S(1)}, f32[2048,128]{1,0:T(8,128)S(1)}) custom-call(bf16[1024,2048]{1,0:T(8,128)(2,1)S(1)} %copy-done, s32[2048,1024]{1,0:T(8,128)} %codes.1, s32[1024]{0:T(1024)S(1)} %copy-done.1), custom_call_target="tpu_custom_call" | custom-call | tf_op jit(solution)/shard_map/pallas_call | solution.py:382
  74.2 0.7 copy.7
  74.9 1.0 %copy.8 = f32[2048,128]{1,0:T(8,128)} copy(f32[2048,128]{1,0:T(8,128)S(1)} %get-tuple-element.5) | data formatting | bytes 2097152
Async XLA Ops:
  0.6 2.2 %copy-start = (bf16[1024,2048]{1,0:T(8,128)(2,1)S(1)}, bf16[1024,2048]{1,0:T(8,128)(2,1)}, u32[]{:S(2)}) copy-start(bf16[1024,2048]{1,0:T(8,128)(2,1)} %ptdf.1) | copy-start | bytes 12582916
  2.8 0.7 copy-start.1

commit v5 on v4

--- a/solution.py
+++ b/solution.py
@@ -9,11 +9,12 @@
 NX, NYL, NYH, NZ, NC = 4, 2, 2, 8, 2
 LANES = 128
 UNITS = 8
-ORDER = (0, 1, 2, 4, 6, 3, 5, 7)
+PARTS = 8
+ORDER = (0, 1, 2, 4, 3, 5, 6, 7)
 LAGS = (1, 3, 5, 7, 9, 10)
 MATMULS = (0, 1, 2, 4)
 RELAY_DELAY = (0, 0)
-PAIR_DELAY = 2
+PAIR_DELAY = 1
 F32, BF16 = jnp.float32, jnp.bfloat16
 
 
@@ -30,9 +31,9 @@
 def kernel(
     ptdf, codes, limit_codes, penalty_out, sens_out,
     p_v, codes_v, inj_v, limit_s, limits, part, core_in, y_out, y_in, z_out, z_in, z_own, adj, pen_v, s_v,
-    opp_out, opp_in, right_out, left_out, right_in, left_in, pair_out, pair_in, sens_v,
+    opp_out, opp_in, right_out, left_out, right_in, left_in, pair_out, pair_in,
     p_sem, c_sem, l_sem, core_sem, y_sem, zs_sem, zr_sem, gzs_sem, gzr_sem, gy_sem, gc_sem,
-    opp_sem, right_sem, left_sem, pair_sem, pen_sem, sens_sem,
+    opp_sem, right_sem, left_sem, pair_sem, pen_sem,
 ):
     br, bus = lax.axis_index("br"), lax.axis_index("bus")
     x, ylo = lax.rem(br, NX), br // NX
@@ -74,11 +75,15 @@
     def codes_copy(u):
         return pltpu.make_async_copy(codes.at[:, columns(u)], codes_v.at[u], c_sem.at[u])
 
-    p_copy = pltpu.make_async_copy(ptdf, p_v, p_sem)
+    def p_copy(i):
+        at = pl.ds(i * (rows // PARTS), rows // PARTS)
+        return pltpu.make_async_copy(ptdf.at[at], p_v.at[at], p_sem.at[i])
+
     limit_copy = pltpu.make_async_copy(limit_codes, limit_s, l_sem)
     codes_copy(jnp.int32(0)).start()
     codes_copy(jnp.int32(1)).start()
-    p_copy.start()
+    for i in range(PARTS):
+        p_copy(i).start()
     limit_copy.start()
     barrier = pltpu.get_barrier_semaphore()
     for device in partners:
@@ -107,10 +112,9 @@
         rows_of = adj.at[u, h, :, core]
         return remote(rows_of, rows_of, gy_sem.at[0, u], gy_sem.at[1, u], far_y)
 
-    def gc_copy(u, near, c):
-        rows_of = adj.at[u, yhi if near else 1 - yhi, :, c]
-        which = 0 if near else 1
-        return remote(rows_of, rows_of, gc_sem.at[0, u, which], gc_sem.at[1, u, which], sibling)
+    def gc_copy(u, c):
+        rows_of = adj.at[u, :, :, c]
+        return remote(rows_of, rows_of, gc_sem.at[0, u], gc_sem.at[1, u], sibling)
 
     def pen_copy(u):
         return pltpu.make_async_copy(pen_v.at[u], penalty_out.at[:, columns(u)], pen_sem.at[u])
@@ -130,7 +134,8 @@
         lax.fori_loop(0, buses // strip, convert, 0)
         @pl.when(k == 0)
         def _():
-            p_copy.wait()
+            for i in range(PARTS):
+                p_copy(i).wait()
             for u in range(2, UNITS):
                 codes_copy(jnp.int32(u)).start()
 
@@ -179,11 +184,10 @@
     def stage_gather_z(u):
         all_z(u, gzs_sem, gzr_sem).wait_recv()
         gy_copy(u, yhi).start()
-        gc_copy(u, True, core).start()
 
     def stage_gather_y(u):
         gy_copy(u, 1 - yhi).wait_recv()
-        gc_copy(u, False, core).start()
+        gc_copy(u, core).start()
 
     def opp_copy(s, side, j):
         return remote(
@@ -201,8 +205,7 @@
         return pl.ds(pl.multiple_of(i * tile, tile), tile)
 
     def stage_sens(u):
-        gc_copy(u, True, 1 - core).wait_recv()
-        gc_copy(u, False, 1 - core).wait_recv()
+        gc_copy(u, 1 - core).wait_recv()
         k, s = u // 2, lax.rem(u, 2)
         rhs = adj[u].reshape(rows, LANES)
         s_v[u] = lax.dot_general(p_v[...], rhs, (((0,), (0,)), ((), ())), preferred_element_type=F32)
@@ -246,9 +249,6 @@
     def pair_copy(i):
         return remote(pair_out.at[i], pair_in.at[i], pair_sem.at[0, i], pair_sem.at[1, i], pair)
 
-    def sens_copy(i):
-        return pltpu.make_async_copy(sens_v.at[i], sens_out.at[tile_at(i)], sens_sem.at[i])
-
     def x_sum(s, i):
         right_copy(s, i).wait_recv()
         left_copy(s, i).wait_recv()
@@ -264,8 +264,7 @@
         for i in (j, steps + j):
             total = x_sum(1, i)
             pair_copy(i).wait_recv()
-            sens_v[i] = total + pair_in[i].astype(F32)
-            sens_copy(i).start()
+            sens_out[tile_at(i)] = total + pair_in[i].astype(F32)
         return 0
 
     waits = {unit: ORDER.index(unit) + LAGS[-1] for unit in range(UNITS)}
@@ -303,8 +302,7 @@
         core_copy(u).wait_send()
         y_copy(u).wait_send()
         gy_copy(u, yhi).wait_send()
-        gc_copy(u, True, core).wait_send()
-        gc_copy(u, False, core).wait_send()
+        gc_copy(u, core).wait_send()
         all_z(u, zs_sem, zr_sem).wait_send()
         all_z(u, gzs_sem, gzr_sem).wait_send()
         pen_copy(u).wait()
@@ -320,7 +318,6 @@
                 right_copy(s, i).wait_send()
                 left_copy(s, i).wait_send()
             pair_copy(i).wait_send()
-            sens_copy(i).wait()
         return 0
 
     lax.fori_loop(0, steps, drain, 0)
@@ -330,7 +327,7 @@
     rows, buses = ptdf.shape
     hours = load_codes.shape[1]
     own = rows // (NYH * NZ * NC)
-    tile = 512
+    tile = 1024
     steps = buses // 2 // tile
     dma = pltpu.SemaphoreType.DMA
     piece = (UNITS, NZ, own, LANES)
@@ -359,8 +356,7 @@
         pltpu.VMEM(tiles, BF16),
         pltpu.VMEM(tiles[1:], BF16),
         pltpu.VMEM(tiles[1:], BF16),
-        pltpu.VMEM(tiles[1:], F32),
-        dma,
+        dma((PARTS,)),
         dma((UNITS,)),
         dma,
         dma((2, UNITS)),
@@ -370,13 +366,12 @@
         dma((UNITS,)),
         dma((UNITS,)),
         dma((2, UNITS)),
-        dma((2, UNITS, 2)),
+        dma((2, UNITS)),
         dma((2, 2, 2, steps)),
         dma((2, 2, 2 * steps)),
         dma((2, 2, 2 * steps)),
         dma((2, 2 * steps)),
         dma((UNITS,)),
-        dma((2 * steps,)),
     ]
     anywhere = pl.BlockSpec(memory_space=pl.ANY)
     return pl.pallas_call(
@@ -386,7 +381,7 @@
             jax.ShapeDtypeStruct((buses, LANES), F32),
         ),
         in_specs=[anywhere] * 3,
-        out_specs=(anywhere, anywhere),
+        out_specs=(anywhere, pl.BlockSpec(memory_space=pltpu.VMEM)),
         scratch_shapes=scratch,
         compiler_params=pltpu.CompilerParams(
             collective_id=0, has_side_effects=True, vmem_limit_bytes=42 * 1024 * 1024

time: 77 us -> 77 us (level); the launches traced: 75.9 us -> 76.8 us
  Pallas kernels: 70.7 us -> 71.7 us
    pallas_call x1, Pallas kernels: 70.7 us -> 71.7 us  [local(): pl.pallas_call(kernel, out_shape=(jax.ShapeDtypeStruct((own, hours), F32)...]
where the time goes in v5:
time: 77 us; the launch traced here: 76.8 us
  Pallas kernels  71.7 us (93%)
  local copies, waits for them, and re-layouts  4.49 us (6%)
    pallas_call x1, Pallas kernels, local(): pl.pallas_call(kernel, out_shape=(jax.ShapeDtypeStruct((own, hours), F32)...  71.7 us
    unnamed x6, local copies, waits for them, and re-layouts  4.49 us

profile of v5, /device:TPU:8, one launch (start us, length us, event | category | flops | bytes accessed | tf_op | source)
XLA Modules:
  0.0 76.8 jit_solution(2230824984217657807)
XLA Ops:
  0.6 0.0 copy-start
  0.6 2.2 %copy-done = bf16[1024,2048]{1,0:T(8,128)(2,1)S(1)} copy-done((bf16[1024,2048]{1,0:T(8,128)(2,1)S(1)}, bf16[1024,2048]{1,0:T(8,128)(2,1)}, u32[]{:S(2)}) %copy-start) | copy-done | bytes 4194328
  2.8 0.0 copy-start.1
  2.8 0.7 copy-done.1
  3.5 71.7 %shard_map.50 = (f32[32,1024]{1,0:T(8,128)S(1)}, f32[2048,128]{1,0:T(8,128)S(1)}) custom-call(bf16[1024,2048]{1,0:T(8,128)(2,1)S(1)} %copy-done, s32[2048,1024]{1,0:T(8,128)} %codes.1, s32[1024]{0:T(1024)S(1)} %copy-done.1), custom_call_target="tpu_custom_call" | custom-call | tf_op jit(solution)/shard_map/pallas_call | solution.py:377
  75.2 0.7 copy.7
  75.9 1.0 %copy.8 = f32[2048,128]{1,0:T(8,128)} copy(f32[2048,128]{1,0:T(8,128)S(1)} %get-tuple-element.5) | data formatting | bytes 2097152
Async XLA Ops:
  0.6 2.2 %copy-start = (bf16[1024,2048]{1,0:T(8,128)(2,1)S(1)}, bf16[1024,2048]{1,0:T(8,128)(2,1)}, u32[]{:S(2)}) copy-start(bf16[1024,2048]{1,0:T(8,128)(2,1)} %ptdf.1) | copy-start | bytes 12582916
  2.8 0.7 copy-start.1
